TPU v7x, 512 devices: a whole 4x4x16 slice. The times are simulated.
512 devices in a mesh: segment: 4 (over z_hi, core), expert: 128 (over y, x, z_lo).
Axes of the slice: x: 4, y: 4, z: 16 (z_hi: 2, z_lo: 8; z = z_hi * 8 + z_lo), core: 2. Of those that a mesh axis runs over, the one named last changes fastest.
Arguments:
- fwd_input: bfloat16 [4, 8192, 1024], P('segment', 'expert'), may hold values from -6 to 6
- fwd_routes: int32 [4, 8192, 8], P('segment', 'expert'), may hold values from 0 to 127, all different within a row; in each aligned block of 64 rows (0 to 63, 64 to 127, ..., all dimensions but the last counted through in order) at most 4 rows name the same one
- fwd_gates: float32 [4, 8192, 8], P('segment', 'expert'), may hold values from 0.05 to 0.3
- bwd_input: bfloat16 [4, 8192, 1024], P('segment', 'expert'), may hold values from -6 to 6
- bwd_grad: bfloat16 [4, 8192, 1024], P('segment', 'expert'), may hold values from -6 to 6
- bwd_routes: int32 [4, 8192, 8], P('segment', 'expert'), may hold values from 0 to 127, all different within a row; in each aligned block of 64 rows (0 to 63, 64 to 127, ..., all dimensions but the last counted through in order) at most 4 rows name the same one
- bwd_gates: float32 [4, 8192, 8], P('segment', 'expert'), may hold values from 0.05 to 0.3
- norm_gain: float32 [4, 1024], P('segment'), may hold values from 0.25 to 1.75
- w_gate: bfloat16 [4, 128, 1024, 768], P('segment', 'expert'), may hold values from -0.1875 to 0.1875
- w_up: bfloat16 [4, 128, 1024, 768], P('segment', 'expert'), may hold values from -0.1875 to 0.1875
- w_down: bfloat16 [4, 128, 768, 1024], P('segment', 'expert'), may hold values from -0.21875 to 0.21875
Outputs:
- fwd_out: bfloat16 [4, 8192, 1024], P('segment', 'expert')
- bwd_out: bfloat16 [4, 8192, 1024], P('segment', 'expert')
Inputs may be any that keep to these rules, and one draw needn't show every extreme that they name: `fwd_routes`: each token names 8 different experts; within the 64 rows of one device (aligned blocks) no expert is named by more than 4 rows, a bound that some block reaches. `bwd_routes`: as for fwd_routes.
All inputs are finite; a program needn't handle non-finite values.
Results may differ from a plain program's by a relative error of at most 0.0051.
Values may be sent and summed in bfloat16 or wider, within the bound.
A program may use at most 64 MiB of HBM per device.

v0:
```python
import jax
import jax.numpy as jnp
from jax import lax
from jax.sharding import PartitionSpec as P

EPSILON = 1e-06


def passed_along(block, axis, distance):
    devices = range(lax.axis_size(axis))
    route = [((i - distance) % len(devices), i) for i in devices]
    return lax.ppermute(block, axis, route)


def norm_scale(stream):
    return lax.rsqrt(jnp.mean(stream * stream, axis=-1, keepdims=True) + EPSILON)


def slot_target(routes, capacity, experts):
    flat_routes = routes.reshape(-1)
    onehot = (flat_routes[:, None] == jnp.arange(experts, dtype=jnp.int32)[None, :]).astype(
        jnp.int32
    )
    before = jnp.cumsum(onehot, axis=0) - onehot
    position = jnp.sum(before * onehot, axis=1)
    return flat_routes * capacity + position


def to_slots(values, target, experts, capacity):
    width = values.shape[-1]
    buffer = jnp.zeros((experts * capacity, width), values.dtype).at[target].set(values)
    return buffer.reshape(experts, capacity, width)


def transposed(left, right):
    return lax.dot_general(
        left, right, (((1,), (1,)), ((), ())), preferred_element_type=jnp.float32
    )


def expert_forward(inputs, gate_matrix, up_matrix, down_matrix):
    token_rows = inputs.reshape(-1, inputs.shape[-1])
    gate = jnp.dot(token_rows, gate_matrix, preferred_element_type=jnp.float32)
    upward = jnp.dot(token_rows, up_matrix, preferred_element_type=jnp.float32)
    hidden = (gate * jax.nn.sigmoid(gate) * upward).astype(jnp.bfloat16)
    result = jnp.dot(hidden, down_matrix, preferred_element_type=jnp.float32).astype(jnp.bfloat16)
    return result.reshape(inputs.shape)


def expert_backward(inputs, grads, gate_matrix, up_matrix, down_matrix):
    token_rows = inputs.reshape(-1, inputs.shape[-1])
    grad_rows = grads.reshape(-1, grads.shape[-1])
    gate = jnp.dot(token_rows, gate_matrix, preferred_element_type=jnp.float32)
    upward = jnp.dot(token_rows, up_matrix, preferred_element_type=jnp.float32)
    d_hidden = transposed(grad_rows, down_matrix)
    sigma = jax.nn.sigmoid(gate)
    d_gate = (d_hidden * upward * sigma * (1.0 + gate * (1.0 - sigma))).astype(jnp.bfloat16)
    d_up = (d_hidden * gate * sigma).astype(jnp.bfloat16)
    result = (transposed(d_gate, gate_matrix) + transposed(d_up, up_matrix)).astype(jnp.bfloat16)
    return result.reshape(inputs.shape)


def on_device(
    fwd_input,
    fwd_routes,
    fwd_gates,
    bwd_input,
    bwd_grad,
    bwd_routes,
    bwd_gates,
    norm_gain,
    w_gate,
    w_up,
    w_down,
):
    experts = lax.axis_size("expert")
    tokens_here = fwd_input.shape[1]
    width = fwd_input.shape[2]
    top_count = fwd_routes.shape[2]
    capacity = min(tokens_here, tokens_here * top_count // experts)
    gain = norm_gain[0]
    gate_matrix = w_gate[0, 0]
    up_matrix = w_up[0, 0]
    down_matrix = w_down[0, 0]
    fwd_stream = fwd_input[0].astype(jnp.float32)
    fwd_normed = (fwd_stream * norm_scale(fwd_stream) * gain).astype(jnp.bfloat16)
    fwd_target = slot_target(fwd_routes[0], capacity, experts)
    fwd_send = to_slots(jnp.repeat(fwd_normed, top_count, axis=0), fwd_target, experts, capacity)
    bwd_stream = bwd_input[0].astype(jnp.float32)
    bwd_scale = norm_scale(bwd_stream)
    bwd_normed = (bwd_stream * bwd_scale * gain).astype(jnp.bfloat16)
    grad_stream = bwd_grad[0].astype(jnp.float32)
    scaled = (
        (bwd_gates[0][:, :, None] * grad_stream[:, None, :]).astype(jnp.bfloat16).reshape(-1, width)
    )
    bwd_target = slot_target(bwd_routes[0], capacity, experts)
    bwd_rows = to_slots(jnp.repeat(bwd_normed, top_count, axis=0), bwd_target, experts, capacity)
    bwd_grads = to_slots(scaled, bwd_target, experts, capacity)
    fwd_result = expert_forward(
        lax.all_to_all(fwd_send, "expert", split_axis=0, concat_axis=0, tiled=True),
        gate_matrix,
        up_matrix,
        down_matrix,
    )
    fwd_back = lax.all_to_all(fwd_result, "expert", split_axis=0, concat_axis=0, tiled=True)
    bwd_result = expert_backward(
        lax.all_to_all(bwd_rows, "expert", split_axis=0, concat_axis=0, tiled=True),
        lax.all_to_all(bwd_grads, "expert", split_axis=0, concat_axis=0, tiled=True),
        gate_matrix,
        up_matrix,
        down_matrix,
    )
    bwd_back = lax.all_to_all(bwd_result, "expert", split_axis=0, concat_axis=0, tiled=True)
    fwd_picked = (
        fwd_back.reshape(-1, width)[fwd_target]
        .reshape(tokens_here, top_count, width)
        .astype(jnp.float32)
    )
    layer_out = (fwd_stream + jnp.sum(fwd_gates[0][:, :, None] * fwd_picked, axis=1)).astype(
        jnp.bfloat16
    )
    bwd_picked = (
        bwd_back.reshape(-1, width)[bwd_target]
        .reshape(tokens_here, top_count, width)
        .astype(jnp.float32)
    )
    summed = gain * jnp.sum(bwd_picked, axis=1)
    inner = jnp.mean(summed * bwd_stream, axis=-1, keepdims=True)
    d_input = (
        grad_stream + bwd_scale * summed - bwd_stream * bwd_scale * bwd_scale * bwd_scale * inner
    ).astype(jnp.bfloat16)
    forward_next = passed_along(layer_out[None], "segment", 1)
    backward_next = passed_along(d_input[None], "segment", -1)
    return (forward_next, backward_next)


def solution(mesh):
    placed = (
        P("segment", "expert", None),
        P("segment", "expert", None),
        P("segment", "expert", None),
        P("segment", "expert", None),
        P("segment", "expert", None),
        P("segment", "expert", None),
        P("segment", "expert", None),
        P("segment", None),
        P("segment", "expert", None, None),
        P("segment", "expert", None, None),
        P("segment", "expert", None, None),
    )
    return jax.shard_map(
        on_device,
        mesh=mesh,
        in_specs=placed,
        out_specs=(P("segment", "expert", None), P("segment", "expert", None)),
        check_vma=False,
    )
```

profile of v0, /device:TPU:1, one launch (start us, length us, event | category | flops | bytes accessed | tf_op | source)
XLA Modules:
  0.0 394.0 jit_solution(10353405192065917419)
XLA Ops:
  3.6 2.8 scatter_custom_fusion.2
  6.4 1.2 reshape.265
  7.6 20.5 %all-to-all-start.3 = ((bf16[128,4,1024]{2,1,0:T(4,128)(2,1)}), bf16[128,4,1024]{2,1,0:T(4,128)(2,1)S(1)}, u32[]{:S(2)}, u32[]{:S(2)}) async-start(bf16[128,4,1024]{2,1,0:T(4,128)(2,1)} %reshape.265), calls=%async_computation.3 | async-start | bytes 2097152 | tf_op jit(solution)/shard_map/all_to_all | solution.py:107
  28.4 3.6 scatter_custom_fusion.1
  32.0 2.3 reshape.262
  34.2 47.5 %all-to-all-done.3 = bf16[128,4,1024]{2,1,0:T(4,128)(2,1)S(1)} async-done(((bf16[128,4,1024]{2,1,0:T(4,128)(2,1)}), bf16[128,4,1024]{2,1,0:T(4,128)(2,1)S(1)}, u32[]{:S(2)}, u32[]{:S(2)}) %all-to-all-start.3) | async-done | bytes 1048608 | tf_op jit(solution)/shard_map/all_to_all | solution.py:107
  81.7 9.1 %all-to-all-start.2 = ((bf16[128,4,1024]{2,1,0:T(4,128)(2,1)}), bf16[128,4,1024]{2,1,0:T(4,128)(2,1)}, u32[]{:S(2)}, u32[]{:S(2)}) async-start(bf16[128,4,1024]{2,1,0:T(4,128)(2,1)} %reshape.262), calls=%async_computation.2 | async-start | bytes 2097152 | tf_op jit(solution)/shard_map/all_to_all | solution.py:108
  91.9 3.9 fusion.13
  95.8 47.9 %all-to-all-done.2 = bf16[128,4,1024]{2,1,0:T(4,128)(2,1)} async-done(((bf16[128,4,1024]{2,1,0:T(4,128)(2,1)}), bf16[128,4,1024]{2,1,0:T(4,128)(2,1)}, u32[]{:S(2)}, u32[]{:S(2)}) %all-to-all-start.2) | async-done | bytes 1048608 | tf_op jit(solution)/shard_map/all_to_all | solution.py:108
  143.7 2.2 reshape.263
  145.9 4.0 %fusion.2 = f32[512,768]{1,0:T(8,128)} fusion(bf16[512,1024]{1,0:T(8,128)(2,1)} %reshape.263, bf16[1,1,768,1024]{3,2,1,0:T(8,128)(2,1)} %param.21), kind=kOutput, calls=%fused_computation.11 | convolution fusion | flops 805306368 | bytes 4194304 | tf_op jit(solution)/shard_map/dot_general | solution.py:36
  149.9 6.1 %fusion.11 = f32[512,1024]{1,0:T(8,128)} fusion(bf16[1,1,1024,768]{3,2,1,0:T(8,128)(2,1)} %param.19, f32[512,768]{1,0:T(8,128)} %fusion.13, f32[512,768]{1,0:T(8,128)} %fusion.2, bf16[512,1024]{1,0:T(8,128)(2,1)S(1)} %copy-done.3, bf16[1,1,1024,768]{3,2,1,0:T(8,128)(2,1)S(1)} %copy-done), kind=kOutput, calls=%fused_computation.20 | convolution fusion | flops 1614544896 | bytes 9437184 | tf_op jit(solution)/shard_map/dot_general | solution.py:36
  156.0 3.6 add_convert_fusion
  159.5 1.2 reshape.267
  160.8 9.0 %all-to-all-start.4 = ((bf16[128,4,1024]{2,1,0:T(4,128)(2,1)}), bf16[128,4,1024]{2,1,0:T(4,128)(2,1)}, u32[]{:S(2)}, u32[]{:S(2)}) async-start(bf16[128,4,1024]{2,1,0:T(4,128)(2,1)} %reshape.267), calls=%async_computation.4 | async-start | bytes 2097152 | tf_op jit(solution)/shard_map/all_to_all | solution.py:113
  171.1 51.7 %all-to-all-done.4 = bf16[128,4,1024]{2,1,0:T(4,128)(2,1)} async-done(((bf16[128,4,1024]{2,1,0:T(4,128)(2,1)}), bf16[128,4,1024]{2,1,0:T(4,128)(2,1)}, u32[]{:S(2)}, u32[]{:S(2)}) %all-to-all-start.4) | async-done | bytes 1048608 | tf_op jit(solution)/shard_map/all_to_all | solution.py:113
  222.8 1.3 reshape.268
  224.1 2.8 gather_fusion.1
  226.9 1.9 convert_reduce_fusion
  229.0 2.8 scatter_custom_fusion
  233.0 61.9 %all_to_all.25 = bf16[128,4,1024]{2,1,0:T(4,128)(2,1)S(1)} all-to-all(bf16[128,4,1024]{2,1,0:T(4,128)(2,1)} %reshape.257), channel_id=1, replica_groups=mesh['segment'=4,'expert'=128] {'expert'}, dimensions={0} | all-to-all | bytes 2097152 | tf_op jit(solution)/shard_map/all_to_all | solution.py:100
  295.9 3.9 %fusion.15 = f32[512,768]{1,0:T(8,128)} fusion(bf16[512,1024]{1,0:T(8,128)(2,1)} %reshape.258, bf16[1,1,1024,768]{3,2,1,0:T(8,128)(2,1)} %param.19), kind=kOutput, calls=%fused_computation.24 | convolution fusion | flops 805306368 | bytes 4194304 | tf_op jit(solution)/shard_map/dot_general | solution.py:43
  299.9 5.2 %fusion.17 = bf16[512,1024]{1,0:T(8,128)(2,1)} fusion(bf16[1,1,768,1024]{3,2,1,0:T(8,128)(2,1)} %param.21, f32[512,768]{1,0:T(8,128)} %fusion.15, bf16[512,1024]{1,0:T(8,128)(2,1)S(1)} %copy-done.4, bf16[1,1,1024,768]{3,2,1,0:T(8,128)(2,1)S(1)} %copy-done), kind=kOutput, calls=%fused_computation.30 | convolution fusion | flops 1613496320 | bytes 6815744 | tf_op jit(solution)/shard_map/dot_general | solution.py:46
  305.1 2.3 reshape.259
  307.3 9.0 %all-to-all-start.1 = ((bf16[128,4,1024]{2,1,0:T(4,128)(2,1)}), bf16[128,4,1024]{2,1,0:T(4,128)(2,1)}, u32[]{:S(2)}, u32[]{:S(2)}) async-start(bf16[128,4,1024]{2,1,0:T(4,128)(2,1)} %reshape.259), calls=%async_computation.1 | async-start | bytes 2097152 | tf_op jit(solution)/shard_map/all_to_all | solution.py:105
  316.5 3.8 collective-permute-start.1
  320.3 54.6 %all-to-all-done.1 = bf16[128,4,1024]{2,1,0:T(4,128)(2,1)} async-done(((bf16[128,4,1024]{2,1,0:T(4,128)(2,1)}), bf16[128,4,1024]{2,1,0:T(4,128)(2,1)}, u32[]{:S(2)}, u32[]{:S(2)}) %all-to-all-start.1) | async-done | bytes 1048608 | tf_op jit(solution)/shard_map/all_to_all | solution.py:105
  374.9 1.3 reshape.260
  376.2 2.8 gather_fusion
  379.0 1.9 fusion
  381.0 9.8 %collective-permute-start = (bf16[1,64,1024]{2,1,0:T(8,128)(2,1)S(1)}, bf16[1,64,1024]{2,1,0:T(8,128)(2,1)S(1)}, u32[]{:S(2)}, u32[]{:S(2)}) collective-permute-start(bf16[1,64,1024]{2,1,0:T(8,128)(2,1)S(1)} %fusion.52), channel_id=1, source_target_pairs={{384,0},{0,128},{128,256},{256,384},{385,1},{1,129},{129,257},{257... | collective-permute-start | bytes 393224 | tf_op jit(solution)/shard_map/ppermute | solution.py:12
  390.8 1.9 collective-permute-done
  (73 shorter events, 9.5 us)
Async XLA Ops:
  0.6 149.3 %copy-start = (bf16[1,1,1024,768]{3,2,1,0:T(8,128)(2,1)S(1)}, bf16[1,1,1024,768]{3,2,1,0:T(8,128)(2,1)}, u32[]{:S(2)}) copy-start(bf16[1,1,1024,768]{3,2,1,0:T(8,128)(2,1)} %param.20) | copy-start | bytes 4718596
  0.6 2.4 copy-start.1
  0.7 2.8 copy-start.6
  6.4 21.8 %copy-start.8 = (f32[1,64,8]{1,2,0:T(8,128)S(1)}, f32[1,64,8]{1,2,0:T(8,128)}, u32[]{:S(2)}) copy-start(f32[1,64,8]{1,2,0:T(8,128)} %param.17) | copy-start | bytes 6148
  7.6 20.7 %copy-start.5 = (bf16[1,64,1024]{2,1,0:T(8,128)(2,1)S(1)}, bf16[1,64,1024]{2,1,0:T(8,128)(2,1)}, u32[]{:S(2)}) copy-start(bf16[1,64,1024]{2,1,0:T(8,128)(2,1)} %param.15) | copy-start | bytes 393220
  7.6 74.1 %all-to-all-start.3 = ((bf16[128,4,1024]{2,1,0:T(4,128)(2,1)}), bf16[128,4,1024]{2,1,0:T(4,128)(2,1)S(1)}, u32[]{:S(2)}, u32[]{:S(2)}) async-start(bf16[128,4,1024]{2,1,0:T(4,128)(2,1)} %reshape.265), calls=%async_computation.3 | async-start | bytes 2097152 | tf_op jit(solution)/shard_map/all_to_all | solution.py:107
  81.7 62.0 %all-to-all-start.2 = ((bf16[128,4,1024]{2,1,0:T(4,128)(2,1)}), bf16[128,4,1024]{2,1,0:T(4,128)(2,1)}, u32[]{:S(2)}, u32[]{:S(2)}) async-start(bf16[128,4,1024]{2,1,0:T(4,128)(2,1)} %reshape.262), calls=%async_computation.2 | async-start | bytes 2097152 | tf_op jit(solution)/shard_map/all_to_all | solution.py:108
  145.9 4.0 %copy-start.3 = (bf16[512,1024]{1,0:T(8,128)(2,1)S(1)}, bf16[512,1024]{1,0:T(8,128)(2,1)}, u32[]{:S(2)}) copy-start(bf16[512,1024]{1,0:T(8,128)(2,1)} %reshape.266) | copy-start | bytes 3145732
  160.8 9.0 %copy-start.7 = (s32[1,64,8]{1,2,0:T(8,128)S(1)}, s32[1,64,8]{1,2,0:T(8,128)}, u32[]{:S(2)}) copy-start(s32[1,64,8]{1,2,0:T(8,128)} %param.12) | copy-start | bytes 6148
  160.8 9.9 %copy-start.2 = (bf16[1,64,1024]{2,1,0:T(8,128)(2,1)S(1)}, bf16[1,64,1024]{2,1,0:T(8,128)(2,1)}, u32[]{:S(2)}) copy-start(bf16[1,64,1024]{2,1,0:T(8,128)(2,1)} %param.11) | copy-start | bytes 393220
  160.8 62.0 %all-to-all-start.4 = ((bf16[128,4,1024]{2,1,0:T(4,128)(2,1)}), bf16[128,4,1024]{2,1,0:T(4,128)(2,1)}, u32[]{:S(2)}, u32[]{:S(2)}) async-start(bf16[128,4,1024]{2,1,0:T(4,128)(2,1)} %reshape.267), calls=%async_computation.4 | async-start | bytes 2097152 | tf_op jit(solution)/shard_map/all_to_all | solution.py:113
  295.9 3.9 %copy-start.4 = (bf16[512,1024]{1,0:T(8,128)(2,1)S(1)}, bf16[512,1024]{1,0:T(8,128)(2,1)}, u32[]{:S(2)}) copy-start(bf16[512,1024]{1,0:T(8,128)(2,1)} %reshape.258) | copy-start | bytes 3145732
  307.3 9.0 %copy-start.9 = (f32[1,64,8]{1,2,0:T(8,128)S(1)}, f32[1,64,8]{1,2,0:T(8,128)}, u32[]{:S(2)}) copy-start(f32[1,64,8]{1,2,0:T(8,128)} %param.13) | copy-start | bytes 6148
  307.3 67.5 %all-to-all-start.1 = ((bf16[128,4,1024]{2,1,0:T(4,128)(2,1)}), bf16[128,4,1024]{2,1,0:T(4,128)(2,1)}, u32[]{:S(2)}, u32[]{:S(2)}) async-start(bf16[128,4,1024]{2,1,0:T(4,128)(2,1)} %reshape.259), calls=%async_computation.1 | async-start | bytes 2097152 | tf_op jit(solution)/shard_map/all_to_all | solution.py:105
  316.5 74.2 %collective-permute-start.1 = (bf16[1,64,1024]{2,1,0:T(8,128)(2,1)S(1)}, bf16[1,64,1024]{2,1,0:T(8,128)(2,1)S(1)}, u32[]{:S(2)}, u32[]{:S(2)}) collective-permute-start(bf16[1,64,1024]{2,1,0:T(8,128)(2,1)S(1)} %fusion.54), channel_id=1, source_target_pairs={{128,0},{256,128},{384,256},{0,384},{129,1},{257,129},{385,257},{1... | collective-permute-start | bytes 393224 | tf_op jit(solution)/shard_map/ppermute | solution.py:12
  381.0 11.7 %collective-permute-start = (bf16[1,64,1024]{2,1,0:T(8,128)(2,1)S(1)}, bf16[1,64,1024]{2,1,0:T(8,128)(2,1)S(1)}, u32[]{:S(2)}, u32[]{:S(2)}) collective-permute-start(bf16[1,64,1024]{2,1,0:T(8,128)(2,1)S(1)} %fusion.52), channel_id=1, source_target_pairs={{384,0},{0,128},{128,256},{256,384},{385,1},{1,129},{129,257},{257... | collective-permute-start | bytes 393224 | tf_op jit(solution)/shard_map/ppermute | solution.py:12
where the time goes:
time: 400 us; the launch traced here: 394 us
  waiting for transfers between devices  204 us (51%)
  blocking collectives  61.9 us (15%)
  starting transfers between devices  61 us (15%)
  local copies, waits for them, and re-layouts  30.1 us (8%)
  matrix products  26.6 us (7%)
  other arithmetic  9.88 us (2%)
    all_to_all x1, blocking collectives, on_device(): lax.all_to_all(fwd_send, 'expert', split_axis=0, concat_axis=0, tiled=True)  61.9 us
    all_to_all x1, waiting for transfers between devices, on_device(): lax.all_to_all(fwd_result, 'expert', split_axis=0, concat_axis=0, tiled=T...  54.6 us
    all_to_all x1, waiting for transfers between devices, on_device(): lax.all_to_all(bwd_result, 'expert', split_axis=0, concat_axis=0, tiled=T...  51.7 us
    all_to_all x1, waiting for transfers between devices, on_device(): lax.all_to_all(bwd_grads, 'expert', split_axis=0, concat_axis=0, tiled=True)  47.9 us
    all_to_all x1, waiting for transfers between devices, on_device(): lax.all_to_all(bwd_rows, 'expert', split_axis=0, concat_axis=0, tiled=True)  47.5 us
    all_to_all x1, starting transfers between devices, on_device(): lax.all_to_all(bwd_rows, 'expert', split_axis=0, concat_axis=0, tiled=True)  20.5 us
    dot_general x3, matrix products, transposed(): lax.dot_general(left, right, (((1,), (1,)), ((), ())), preferred_element_...  13.6 us
    ppermute x2, starting transfers between devices, passed_along(): return lax.ppermute(block, axis, route)  13.5 us
  transfers between devices with their start and end apart: 6, of which 5 were waited for; matrix products, arithmetic and copies ran while one was open for 5% of the time, Pallas kernels for 0%

commit v1 on v0

v1 whole, which is shorter than its diff:
```python
import functools
import types

import jax
import jax.numpy as jnp
from jax import lax
from jax.experimental import pallas as pl
from jax.experimental.pallas import tpu as pltpu
from jax.sharding import PartitionSpec as P

EPSILON = 1e-06
MESH = pl.DeviceIdType.MESH
F32 = jnp.float32
BF16 = jnp.bfloat16
LINE = 8
HALVES = 2


def geometry(experts, tokens, top, width, hidden, line):
    g = types.SimpleNamespace()
    g.line = line
    g.plane = experts // line
    g.tokens = tokens
    g.top = top
    g.width = width
    g.hidden = hidden
    g.capacity = tokens * top // experts
    g.sources = line // 2
    g.rows = g.sources * g.capacity
    g.group = g.sources * tokens
    g.chunk = tokens // HALVES
    assert g.plane * g.rows == g.group
    return g


def transposed(left, right):
    return lax.dot_general(left, right, (((1,), (1,)), ((), ())), preferred_element_type=F32)


def picked_back(picks, rows):
    return lax.dot_general(picks, rows, (((0,), (0,)), ((), ())), preferred_element_type=F32)


def kernel(
    g,
    meta_in,
    gain_ref,
    fwd_in,
    bwd_in,
    grad_in,
    gate_hbm,
    up_hbm,
    down_hbm,
    y_ref,
    dx_ref,
    tok,
    meta,
    w_gate,
    w_up,
    w_down,
    picks,
    weighted,
    send,
    recv,
    made,
    back,
    part,
    acc,
    stage,
    load_sem,
    tok_send,
    tok_recv,
    meta_send,
    meta_recv,
    out_send,
    out_recv,
    own_sem,
    sum_send,
    sum_recv,
):
    me = lax.axis_index("expert")
    z = lax.rem(me, g.line)
    here = me // g.line
    half = z // g.sources
    last = g.line - 1

    def expert_at(plane, layer):
        return {"expert": plane * g.line + layer}

    def base_of(group):
        return lax.rem(half + group, 2) * g.sources

    loads = [
        pltpu.make_async_copy(meta_in, meta.at[z], load_sem.at[0]),
        pltpu.make_async_copy(fwd_in, tok.at[0, z], load_sem.at[1]),
        pltpu.make_async_copy(bwd_in, tok.at[1, z], load_sem.at[2]),
        pltpu.make_async_copy(grad_in, tok.at[2, z], load_sem.at[3]),
    ]
    weights = [
        pltpu.make_async_copy(gate_hbm, w_gate, load_sem.at[4]),
        pltpu.make_async_copy(up_hbm, w_up, load_sem.at[5]),
        pltpu.make_async_copy(down_hbm, w_down, load_sem.at[6]),
    ]
    for copy in loads + weights:
        copy.start()

    barrier = pltpu.get_barrier_semaphore()

    @pl.when(z > 0)
    def _():
        pl.semaphore_signal(barrier, inc=1, device_id=expert_at(here, z - 1), device_id_type=MESH)

    @pl.when(z < last)
    def _():
        pl.semaphore_signal(barrier, inc=1, device_id=expert_at(here, z + 1), device_id_type=MESH)

    def greet(k, carry):
        there = lax.rem(here + k, g.plane)
        pl.semaphore_signal(barrier, inc=1, device_id=expert_at(there, z), device_id_type=MESH)
        return carry

    lax.fori_loop(1, g.plane, greet, 0)
    beside = jnp.where(z > 0, 1, 0) + jnp.where(z < last, 1, 0)
    pl.semaphore_wait(barrier, g.plane - 1 + beside)
    for copy in loads:
        copy.wait()

    def tok_copy(array, source, piece, way):
        rows = pl.ds(piece * g.chunk, g.chunk)
        ref = tok.at[array, source, rows]
        return pltpu.make_async_remote_copy(
            src_ref=ref,
            dst_ref=ref,
            send_sem=tok_send.at[way, array, source, piece],
            recv_sem=tok_recv.at[array, source, piece],
            device_id=expert_at(here, z + 1 - 2 * way),
            device_id_type=MESH,
        )

    def meta_copy(source, way):
        ref = meta.at[source]
        return pltpu.make_async_remote_copy(
            src_ref=ref,
            dst_ref=ref,
            send_sem=meta_send.at[way, source],
            recv_sem=meta_recv.at[source],
            device_id=expert_at(here, z + 1 - 2 * way),
            device_id_type=MESH,
        )

    def handed_on(step, make):
        for way in range(2):
            source = z - step if way == 0 else z + step
            inside = source >= 0 if way == 0 else source <= last
            onward = z < last if way == 0 else z > 0

            @pl.when(inside)
            def _():
                @pl.when(step > 0)
                def _():
                    make(source, way).wait_recv()

                @pl.when(onward)
                def _():
                    make(source, way).start()

    def gather_steps(arrays, first, stop):
        def one(step, carry):
            if 0 in arrays:
                handed_on(step, meta_copy)
            for piece in range(HALVES):
                for array in arrays:
                    handed_on(step, lambda source, way: tok_copy(array, source, piece, way))
            return carry

        lax.fori_loop(first, stop, one, 0)

    def make_picks(stream, group):
        base = base_of(group)
        low = lax.broadcasted_iota(jnp.int32, (2 * g.top, 2 * g.tokens), 1) < g.tokens
        pieces = []
        for pair in range(g.sources // 2):
            one, two = meta[base + 2 * pair], meta[base + 2 * pair + 1]
            if stream == 0:
                two = pltpu.roll(two, g.tokens, 1)
            else:
                one = pltpu.roll(one, g.tokens, 1)
            pieces.append(jnp.where(low, one, two))
        table = jnp.concatenate(pieces, axis=1) if len(pieces) > 1 else pieces[0]
        shape = (g.plane, g.group)
        expert = (lax.broadcasted_iota(jnp.int32, shape, 0) * g.line + z).astype(F32)
        chosen = jnp.zeros(shape, F32)
        gates = jnp.zeros(shape, F32)
        for k in range(g.top):
            hit = table[k : k + 1, :] == expert
            chosen = jnp.where(hit, 1.0, chosen)
            gates = jnp.where(hit, table[g.top + k : g.top + k + 1, :], gates)
        square = (g.group, g.group)
        above = lax.broadcasted_iota(jnp.int32, square, 0)
        right = lax.broadcasted_iota(jnp.int32, square, 1)
        earlier = (above < right) & (above // g.tokens == right // g.tokens)
        place = jnp.dot(
            chosen.astype(BF16), jnp.where(earlier, 1.0, 0.0).astype(BF16), preferred_element_type=F32
        )
        lane = lax.broadcasted_iota(jnp.int32, shape, 1) // g.tokens * g.capacity
        code = jnp.where(chosen > 0.0, lane.astype(F32) + place, -1.0)

        def spread(small):
            wide = jnp.broadcast_to(small[:, None, :], (g.plane, g.rows, g.group))
            return wide.reshape(g.group, g.group)

        slot = lax.rem(above, g.rows).astype(F32)
        hit = spread(code) == slot
        picks[stream, group] = jnp.where(hit, 1.0, 0.0).astype(BF16)
        by_row = jnp.where(hit, spread(gates), 0.0)
        if stream == 0:
            high = by_row.astype(BF16)
            weighted[group, 0] = high
            weighted[group, 1] = (by_row - high.astype(F32)).astype(BF16)
            return None
        return jnp.sum(by_row, axis=1, keepdims=True)

    def normed_rows(array, group):
        base = base_of(group)
        rows = tok[array, pl.ds(base, g.sources)].reshape(g.group, g.width).astype(F32)
        scale = lax.rsqrt(jnp.mean(rows * rows, axis=-1, keepdims=True) + EPSILON)
        return (rows * scale * gain_ref[...]).astype(BF16)

    def plane_copy(kind, group, source, target, there):
        slot = 2 * kind + group
        return pltpu.make_async_remote_copy(
            src_ref=source.at[pl.ds(there * g.rows, g.rows)],
            dst_ref=target.at[pl.ds(here * g.rows, g.rows)],
            send_sem=out_send.at[slot],
            recv_sem=out_recv.at[slot],
            device_id=expert_at(there, z),
            device_id_type=MESH,
        )

    def own_copy(kind, group, source, target):
        rows = pl.ds(here * g.rows, g.rows)
        return pltpu.make_async_copy(source.at[rows], target.at[rows], own_sem.at[2 * kind + group])

    def plane_send(kind, group, source, target):
        def one(k, carry):
            there = lax.rem(here + k, g.plane)
            plane_copy(kind, group, source, target, there).start()
            return carry

        lax.fori_loop(1, g.plane, one, 0)
        own_copy(kind, group, source, target).start()

    def all_but_one(kind, group, ref):
        most = ref.at[pl.ds(0, (g.plane - 1) * g.rows)]
        slot = 2 * kind + group
        return pltpu.make_async_remote_copy(
            src_ref=most,
            dst_ref=most,
            send_sem=out_send.at[slot],
            recv_sem=out_recv.at[slot],
            device_id=expert_at(lax.rem(here + 1, g.plane), z),
            device_id_type=MESH,
        )

    def plane_wait(kind, group, source, target):
        all_but_one(kind, group, target).wait_recv()
        own_copy(kind, group, source, target).wait()

    def dispatch_fwd(group):
        make_picks(0, group)
        rows = jnp.dot(picks[0, group], normed_rows(0, group), preferred_element_type=F32)
        send[0, group] = rows.astype(BF16)
        plane_send(0, group, send.at[0, group], recv.at[0, group])

    def dispatch_bwd(group):
        by_row = make_picks(1, group)
        rows = jnp.dot(picks[1, group], normed_rows(1, group), preferred_element_type=F32)
        send[1, group] = rows.astype(BF16)
        plane_send(1, group, send.at[1, group], recv.at[1, group])
        base = base_of(group)
        grads = tok[2, pl.ds(base, g.sources)].reshape(g.group, g.width)
        rows = jnp.dot(picks[1, group], grads, preferred_element_type=F32)
        send[2, group] = (rows * by_row).astype(BF16)
        plane_send(2, group, send.at[2, group], recv.at[2, group])

    def expert_fwd(group):
        plane_wait(0, group, send.at[0, group], recv.at[0, group])
        rows = recv[0, group]
        gate = jnp.dot(rows, w_gate[...], preferred_element_type=F32)
        upward = jnp.dot(rows, w_up[...], preferred_element_type=F32)
        hidden = (gate * jax.nn.sigmoid(gate) * upward).astype(BF16)
        made[0, group] = jnp.dot(hidden, w_down[...], preferred_element_type=F32).astype(BF16)
        plane_send(3, group, made.at[0, group], back.at[0, group])

    def expert_bwd(group):
        plane_wait(1, group, send.at[1, group], recv.at[1, group])
        rows = recv[1, group]
        gate = jnp.dot(rows, w_gate[...], preferred_element_type=F32)
        upward = jnp.dot(rows, w_up[...], preferred_element_type=F32)
        plane_wait(2, group, send.at[2, group], recv.at[2, group])
        d_hidden = transposed(recv[2, group], w_down[...])
        sigma = jax.nn.sigmoid(gate)
        d_gate = (d_hidden * upward * sigma * (1.0 + gate * (1.0 - sigma))).astype(BF16)
        d_up = (d_hidden * gate * sigma).astype(BF16)
        made[1, group] = (transposed(d_gate, w_gate[...]) + transposed(d_up, w_up[...])).astype(BF16)
        plane_send(4, group, made.at[1, group], back.at[1, group])

    def combine(stream, group):
        plane_wait(3 + stream, group, made.at[stream, group], back.at[stream, group])
        rows = back[stream, group]
        if stream == 0:
            total = picked_back(weighted[group, 0], rows) + picked_back(weighted[group, 1], rows)
        else:
            total = picked_back(picks[1, group], rows)
        part[stream, pl.ds(base_of(group), g.sources)] = total.reshape(g.sources, g.tokens, g.width)

    def sum_copy(stream, owner, piece, way):
        rows = pl.ds(piece * g.chunk, g.chunk)
        return pltpu.make_async_remote_copy(
            src_ref=stage.at[stream, owner, rows],
            dst_ref=acc.at[stream, way, owner, rows],
            send_sem=sum_send.at[stream, owner, piece],
            recv_sem=sum_recv.at[stream, way, owner, piece],
            device_id=expert_at(here, z + 1 - 2 * way),
            device_id_type=MESH,
        )

    def sum_steps(stream, first, stop):
        def one(step, carry):
            for piece in range(HALVES):
                rows = pl.ds(piece * g.chunk, g.chunk)
                for way in range(2):
                    owner = last - step if way == 0 else step
                    ahead = owner > z if way == 0 else owner < z
                    behind = z > 0 if way == 0 else z < last

                    @pl.when(ahead & behind)
                    def _():
                        sum_copy(stream, owner, piece, way).wait_recv()
                        total = part[stream, owner, rows] + acc[stream, way, owner, rows].astype(F32)
                        stage[stream, owner, rows] = total.astype(BF16)
                        sum_copy(stream, owner, piece, way).start()

                    @pl.when(ahead & jnp.logical_not(behind))
                    def _():
                        stage[stream, owner, rows] = part[stream, owner, rows].astype(BF16)
                        sum_copy(stream, owner, piece, way).start()

            return carry

        lax.fori_loop(first, stop, one, 0)

    def collected(stream):
        for way in range(2):
            behind = z > 0 if way == 0 else z < last

            @pl.when(behind)
            def _():
                for piece in range(HALVES):
                    sum_copy(stream, z, piece, way).wait_recv()
                part[stream, z] = part[stream, z] + acc[stream, way, z].astype(F32)

        return part[stream, z]

    def finish_fwd():
        y_ref[...] = (tok[0, z].astype(F32) + collected(0)).astype(BF16)

    def finish_bwd():
        summed = gain_ref[...] * collected(1)
        stream = tok[1, z].astype(F32)
        scale = lax.rsqrt(jnp.mean(stream * stream, axis=-1, keepdims=True) + EPSILON)
        inner = jnp.mean(summed * stream, axis=-1, keepdims=True)
        grad = tok[2, z].astype(F32)
        dx_ref[...] = (grad + scale * summed - stream * scale * scale * scale * inner).astype(BF16)

    near = g.sources
    gather_steps((0,), 0, near)
    gather_steps((1, 2), 0, 1)
    dispatch_fwd(0)
    gather_steps((0,), near, g.line)
    dispatch_fwd(1)
    gather_steps((1, 2), 1, 2)
    for copy in weights:
        copy.wait()
    expert_fwd(0)
    gather_steps((1, 2), 2, near)
    dispatch_bwd(0)
    gather_steps((1, 2), near, near + 1)
    expert_fwd(1)
    gather_steps((1, 2), near + 1, near + 2)
    combine(0, 0)
    gather_steps((1, 2), near + 2, near + 3)
    combine(0, 1)
    gather_steps((1, 2), near + 3, g.line)
    dispatch_bwd(1)
    sum_steps(0, 0, 2)
    expert_bwd(0)
    sum_steps(0, 2, 4)
    expert_bwd(1)
    sum_steps(0, 4, last)
    combine(1, 0)
    combine(1, 1)
    sum_steps(1, 0, last)
    finish_fwd()
    finish_bwd()

    for way in range(2):
        onward = z < last if way == 0 else z > 0

        @pl.when(onward)
        def _():
            def left(source, carry):
                sent = source <= z if way == 0 else source >= z

                @pl.when(sent)
                def _():
                    meta_copy(source, way).wait_send()
                    for array in range(3):
                        for piece in range(HALVES):
                            tok_copy(array, source, piece, way).wait_send()

                @pl.when(source > z if way == 0 else source < z)
                def _():
                    for stream in range(2):
                        for piece in range(HALVES):
                            sum_copy(stream, source, piece, way).wait_send()

                return carry

            lax.fori_loop(0, g.line, left, 0)

    for group in range(2):
        for kind in range(3):
            all_but_one(kind, group, send.at[kind, group]).wait_send()
        for stream in range(2):
            all_but_one(3 + stream, group, made.at[stream, group]).wait_send()


def passed_along(block, axis, distance):
    devices = range(lax.axis_size(axis))
    route = [((i - distance) % len(devices), i) for i in devices]
    return lax.ppermute(block, axis, route)


def on_device(
    line,
    fwd_input,
    fwd_routes,
    fwd_gates,
    bwd_input,
    bwd_grad,
    bwd_routes,
    bwd_gates,
    norm_gain,
    w_gate,
    w_up,
    w_down,
):
    _, tokens, width = fwd_input.shape
    top = fwd_routes.shape[2]
    hidden = w_gate.shape[3]
    g = geometry(lax.axis_size("expert"), tokens, top, width, hidden, line)
    routes = jnp.concatenate([fwd_routes[0], bwd_routes[0]], axis=0).astype(F32)
    gates = jnp.concatenate([fwd_gates[0], bwd_gates[0]], axis=0)
    meta = jnp.concatenate([routes, gates], axis=1).T
    block = jax.ShapeDtypeStruct((tokens, width), BF16)
    anywhere = pl.BlockSpec(memory_space=pl.ANY)
    in_vmem = pl.BlockSpec(memory_space=pltpu.VMEM)
    dma = pltpu.SemaphoreType.DMA
    y, dx = pl.pallas_call(
        functools.partial(kernel, g),
        out_shape=(block, block),
        in_specs=[anywhere, in_vmem] + [anywhere] * 6,
        out_specs=(in_vmem, in_vmem),
        scratch_shapes=[
            pltpu.VMEM((3, line, tokens, width), BF16),
            pltpu.VMEM((line, 2 * top, 2 * tokens), F32),
            pltpu.VMEM((width, hidden), BF16),
            pltpu.VMEM((width, hidden), BF16),
            pltpu.VMEM((hidden, width), BF16),
            pltpu.VMEM((2, 2, g.group, g.group), BF16),
            pltpu.VMEM((2, 2, g.group, g.group), BF16),
            pltpu.VMEM((3, 2, g.group, width), BF16),
            pltpu.VMEM((3, 2, g.group, width), BF16),
            pltpu.VMEM((2, 2, g.group, width), BF16),
            pltpu.VMEM((2, 2, g.group, width), BF16),
            pltpu.VMEM((2, line, tokens, width), F32),
            pltpu.VMEM((2, 2, line, tokens, width), BF16),
            pltpu.VMEM((2, line, tokens, width), BF16),
            dma((7,)),
            dma((2, 3, line, HALVES)),
            dma((3, line, HALVES)),
            dma((2, line)),
            dma((line,)),
            dma((10,)),
            dma((10,)),
            dma((10,)),
            dma((2, line, HALVES)),
            dma((2, 2, line, HALVES)),
        ],
        compiler_params=pltpu.CompilerParams(
            collective_id=0, has_side_effects=True, vmem_limit_bytes=56 * 1024 * 1024
        ),
        name="relay_tick",
    )(
        meta,
        norm_gain,
        fwd_input[0],
        bwd_input[0],
        bwd_grad[0],
        w_gate[0, 0],
        w_up[0, 0],
        w_down[0, 0],
    )
    return passed_along(y[None], "segment", 1), passed_along(dx[None], "segment", -1)


def solution(mesh, line=LINE):
    placed = (
        P("segment", "expert", None),
        P("segment", "expert", None),
        P("segment", "expert", None),
        P("segment", "expert", None),
        P("segment", "expert", None),
        P("segment", "expert", None),
        P("segment", "expert", None),
        P("segment", None),
        P("segment", "expert", None, None),
        P("segment", "expert", None, None),
        P("segment", "expert", None, None),
    )
    return jax.shard_map(
        functools.partial(on_device, line),
        mesh=mesh,
        in_specs=placed,
        out_specs=(P("segment", "expert", None), P("segment", "expert", None)),
        check_vma=False,
    )
```

time: 400 us -> 379 us (0.948)
  the two profiles are of different devices: /device:TPU:1 before, /device:TPU:154 now
where the time goes in v1:
time: 379 us; the launch traced here: 378 us
  Pallas kernels  353 us (93%)
  waiting for transfers between devices  16.9 us (4%)
  starting transfers between devices  4.33 us (1%)
    pallas_call x1, Pallas kernels, on_device(): pl.pallas_call(functools.partial(kernel, g), out_shape=(block, block), in...  353 us
    ppermute x2, waiting for transfers between devices, passed_along(): return lax.ppermute(block, axis, route)  16.9 us
  transfers between devices with their start and end apart: 2, of which 2 were waited for; matrix products, arithmetic and copies ran while one was open for 0% of the time, Pallas kernels for 0%

profile of v1, /device:TPU:154, one launch (start us, length us, event | category | flops | bytes accessed | tf_op | source)
XLA Modules:
  0.0 378.3 jit_solution(5561751517562409007)
XLA Ops:
  0.6 0.8 add_convert_fusion
  1.4 1.4 maximum_bitcast_fusion.meta_in
  2.8 353.0 %relay_tick.1 = (bf16[64,1024]{1,0:T(8,128)(2,1)}, bf16[64,1024]{1,0:T(8,128)(2,1)}) custom-call(f32[16,128]{1,0:T(8,128)} %maximum_bitcast_fusion.meta_in, f32[1,1024]{1,0:T(1,128)} %gain_ref.1, bf16[64,1024]{1,0:T(8,128)(2,1)} %bitcast.17, bf16[64,1024]{1,0:T(8,128)(2,1)} %bitcast.18, bf16[64,1024]{1,0:T(8,128)(2,1)} %bitcast.19, ...), custom_call_target="tpu_custom_call" | custom-call | tf_op jit(solution)/shard_map/relay_tick/pallas_call | solution.py:470
  355.8 1.9 collective-permute-start.1
  357.7 2.4 collective-permute-start
  360.1 0.4 collective-permute-done.1
  360.6 16.5 %collective-permute-done = bf16[1,64,1024]{2,1,0:T(8,128)(2,1)S(1)} collective-permute-done((bf16[1,64,1024]{2,1,0:T(8,128)(2,1)}, bf16[1,64,1024]{2,1,0:T(8,128)(2,1)S(1)}, u32[]{:S(2)}, u32[]{:S(2)}) %collective-permute-start) | collective-permute-done | bytes 131104 | tf_op jit(solution)/shard_map/ppermute | solution.py:442
  377.0 0.7 copy.15
  377.7 0.7 copy.16
Async XLA Ops:
  355.8 4.7 %collective-permute-start.1 = (bf16[1,64,1024]{2,1,0:T(8,128)(2,1)}, bf16[1,64,1024]{2,1,0:T(8,128)(2,1)S(1)}, u32[]{:S(2)}, u32[]{:S(2)}) collective-permute-start(bf16[1,64,1024]{2,1,0:T(8,128)(2,1)} %bitcast.25), channel_id=1, source_target_pairs={{128,0},{256,128},{384,256},{0,384},{129,1},{257,129},{385,257},{1... | collective-permute-start | bytes 393224 | tf_op jit(solution)/shard_map/ppermute | solution.py:442
  357.7 19.3 %collective-permute-start = (bf16[1,64,1024]{2,1,0:T(8,128)(2,1)}, bf16[1,64,1024]{2,1,0:T(8,128)(2,1)S(1)}, u32[]{:S(2)}, u32[]{:S(2)}) collective-permute-start(bf16[1,64,1024]{2,1,0:T(8,128)(2,1)} %bitcast.24), channel_id=1, source_target_pairs={{384,0},{0,128},{128,256},{256,384},{385,1},{1,129},{129,257},{257... | collective-permute-start | bytes 393224 | tf_op jit(solution)/shard_map/ppermute | solution.py:442

commit v2 on v1

--- a/solution.py
+++ b/solution.py
@@ -14,6 +14,36 @@
 BF16 = jnp.bfloat16
 LINE = 8
 HALVES = 2
+SCHEDULE = (
+    ("gather", (0,), 0, 4),
+    ("gather", (1, 2), 0, 1),
+    ("dispatch_fwd", 0),
+    ("gather", (0,), 4, 8),
+    ("dispatch_fwd", 1),
+    ("gather", (1, 2), 1, 2),
+    ("weights",),
+    ("expert_fwd", 0),
+    ("gather", (1, 2), 2, 4),
+    ("dispatch_bwd", 0),
+    ("gather", (1, 2), 4, 5),
+    ("expert_fwd", 1),
+    ("gather", (1, 2), 5, 6),
+    ("combine", 0, 0),
+    ("gather", (1, 2), 6, 7),
+    ("combine", 0, 1),
+    ("gather", (1, 2), 7, 8),
+    ("dispatch_bwd", 1),
+    ("sum", 0, 0, 2),
+    ("expert_bwd", 0),
+    ("sum", 0, 2, 4),
+    ("expert_bwd", 1),
+    ("sum", 0, 4, 7),
+    ("combine", 1, 0),
+    ("combine", 1, 1),
+    ("sum", 1, 0, 7),
+    ("finish_fwd",),
+    ("finish_bwd",),
+)
 
 
 def geometry(experts, tokens, top, width, hidden, line):
@@ -330,18 +360,17 @@
             for piece in range(HALVES):
                 rows = pl.ds(piece * g.chunk, g.chunk)
                 for way in range(2):
-                    owner = last - step if way == 0 else step
-                    ahead = owner > z if way == 0 else owner < z
-                    behind = z > 0 if way == 0 else z < last
-
-                    @pl.when(ahead & behind)
+                    from_end = z if way == 0 else last - z
+                    owner = last - (step - from_end) if way == 0 else step - from_end
+
+                    @pl.when((step >= from_end) & (from_end > 0))
                     def _():
                         sum_copy(stream, owner, piece, way).wait_recv()
                         total = part[stream, owner, rows] + acc[stream, way, owner, rows].astype(F32)
                         stage[stream, owner, rows] = total.astype(BF16)
                         sum_copy(stream, owner, piece, way).start()
 
-                    @pl.when(ahead & jnp.logical_not(behind))
+                    @pl.when(from_end == 0)
                     def _():
                         stage[stream, owner, rows] = part[stream, owner, rows].astype(BF16)
                         sum_copy(stream, owner, piece, way).start()
@@ -373,37 +402,27 @@
         grad = tok[2, z].astype(F32)
         dx_ref[...] = (grad + scale * summed - stream * scale * scale * scale * inner).astype(BF16)
 
-    near = g.sources
-    gather_steps((0,), 0, near)
-    gather_steps((1, 2), 0, 1)
-    dispatch_fwd(0)
-    gather_steps((0,), near, g.line)
-    dispatch_fwd(1)
-    gather_steps((1, 2), 1, 2)
-    for copy in weights:
-        copy.wait()
-    expert_fwd(0)
-    gather_steps((1, 2), 2, near)
-    dispatch_bwd(0)
-    gather_steps((1, 2), near, near + 1)
-    expert_fwd(1)
-    gather_steps((1, 2), near + 1, near + 2)
-    combine(0, 0)
-    gather_steps((1, 2), near + 2, near + 3)
-    combine(0, 1)
-    gather_steps((1, 2), near + 3, g.line)
-    dispatch_bwd(1)
-    sum_steps(0, 0, 2)
-    expert_bwd(0)
-    sum_steps(0, 2, 4)
-    expert_bwd(1)
-    sum_steps(0, 4, last)
-    combine(1, 0)
-    combine(1, 1)
-    sum_steps(1, 0, last)
-    finish_fwd()
-    finish_bwd()
-
+    do = {
+        "gather": gather_steps,
+        "sum": sum_steps,
+        "dispatch_fwd": dispatch_fwd,
+        "dispatch_bwd": dispatch_bwd,
+        "expert_fwd": expert_fwd,
+        "expert_bwd": expert_bwd,
+        "combine": combine,
+        "finish_fwd": finish_fwd,
+        "finish_bwd": finish_bwd,
+    }
+    for name, *rest in SCHEDULE:
+        if name == "weights":
+            for copy in weights:
+                copy.wait()
+        else:
+            do[name](*rest)
+
+    names = [entry[0] for entry in SCHEDULE]
+    arrays = sorted({array for entry in SCHEDULE if entry[0] == "gather" for array in entry[1]})
+    streams = sorted({entry[1] for entry in SCHEDULE if entry[0] == "sum"})
     for way in range(2):
         onward = z < last if way == 0 else z > 0
 
@@ -414,14 +433,15 @@
 
                 @pl.when(sent)
                 def _():
-                    meta_copy(source, way).wait_send()
-                    for array in range(3):
+                    if 0 in arrays:
+                        meta_copy(source, way).wait_send()
+                    for array in arrays:
                         for piece in range(HALVES):
                             tok_copy(array, source, piece, way).wait_send()
 
                 @pl.when(source > z if way == 0 else source < z)
                 def _():
-                    for stream in range(2):
+                    for stream in streams:
                         for piece in range(HALVES):
                             sum_copy(stream, source, piece, way).wait_send()
 
@@ -429,11 +449,16 @@
 
             lax.fori_loop(0, g.line, left, 0)
 
-    for group in range(2):
-        for kind in range(3):
-            all_but_one(kind, group, send.at[kind, group]).wait_send()
-        for stream in range(2):
-            all_but_one(3 + stream, group, made.at[stream, group]).wait_send()
+    for name, *rest in SCHEDULE:
+        if name == "dispatch_fwd":
+            all_but_one(0, rest[0], send.at[0, rest[0]]).wait_send()
+        if name == "dispatch_bwd":
+            all_but_one(1, rest[0], send.at[1, rest[0]]).wait_send()
+            all_but_one(2, rest[0], send.at[2, rest[0]]).wait_send()
+        if name == "expert_fwd":
+            all_but_one(3, rest[0], made.at[0, rest[0]]).wait_send()
+        if name == "expert_bwd":
+            all_but_one(4, rest[0], made.at[1, rest[0]]).wait_send()
 
 
 def passed_along(block, axis, distance):

time: 379 us -> 161 us (0.42)
  the two profiles are of different devices: /device:TPU:154 before, /device:TPU:32 now
where the time goes in v2:
time: 161 us; the launch traced here: 160 us
  Pallas kernels  132 us (82%)
  waiting for transfers between devices  20 us (12%)
  starting transfers between devices  4.33 us (3%)
  other arithmetic  2.15 us (1%)
    pallas_call x1, Pallas kernels, on_device(): pl.pallas_call(functools.partial(kernel, g), out_shape=(block, block), in...  132 us
    ppermute x2, waiting for transfers between devices, passed_along(): return lax.ppermute(block, axis, route)  20 us
    ppermute x2, starting transfers between devices, passed_along(): return lax.ppermute(block, axis, route)  4.33 us
  transfers between devices with their start and end apart: 2, of which 2 were waited for; matrix products, arithmetic and copies ran while one was open for 0% of the time, Pallas kernels for 0%

profile of v2, /device:TPU:32, one launch (start us, length us, event | category | flops | bytes accessed | tf_op | source)
XLA Modules:
  0.0 160.3 jit_solution(5243349426349099348)
XLA Ops:
  0.6 0.8 add_convert_fusion
  1.4 1.4 maximum_bitcast_fusion.meta_in
  2.8 131.9 %relay_tick.1 = (bf16[64,1024]{1,0:T(8,128)(2,1)}, bf16[64,1024]{1,0:T(8,128)(2,1)}) custom-call(f32[16,128]{1,0:T(8,128)} %maximum_bitcast_fusion.meta_in, f32[1,1024]{1,0:T(1,128)} %gain_ref.1, bf16[64,1024]{1,0:T(8,128)(2,1)} %bitcast.17, bf16[64,1024]{1,0:T(8,128)(2,1)} %bitcast.18, bf16[64,1024]{1,0:T(8,128)(2,1)} %bitcast.19, ...), custom_call_target="tpu_custom_call" | custom-call | tf_op jit(solution)/shard_map/relay_tick/pallas_call | solution.py:495
  134.7 1.9 %collective-permute-start.1 = (bf16[1,64,1024]{2,1,0:T(8,128)(2,1)}, bf16[1,64,1024]{2,1,0:T(8,128)(2,1)S(1)}, u32[]{:S(2)}, u32[]{:S(2)}) collective-permute-start(bf16[1,64,1024]{2,1,0:T(8,128)(2,1)} %bitcast.25), channel_id=1, source_target_pairs={{128,0},{256,128},{384,256},{0,384},{129,1},{257,129},{385,257},{1... | collective-permute-start | bytes 393224 | tf_op jit(solution)/shard_map/ppermute | solution.py:467
  136.6 2.4 %collective-permute-start = (bf16[1,64,1024]{2,1,0:T(8,128)(2,1)}, bf16[1,64,1024]{2,1,0:T(8,128)(2,1)S(1)}, u32[]{:S(2)}, u32[]{:S(2)}) collective-permute-start(bf16[1,64,1024]{2,1,0:T(8,128)(2,1)} %bitcast.24), channel_id=1, source_target_pairs={{384,0},{0,128},{128,256},{256,384},{385,1},{1,129},{129,257},{257... | collective-permute-start | bytes 393224 | tf_op jit(solution)/shard_map/ppermute | solution.py:467
  139.0 4.6 %collective-permute-done.1 = bf16[1,64,1024]{2,1,0:T(8,128)(2,1)S(1)} collective-permute-done((bf16[1,64,1024]{2,1,0:T(8,128)(2,1)}, bf16[1,64,1024]{2,1,0:T(8,128)(2,1)S(1)}, u32[]{:S(2)}, u32[]{:S(2)}) %collective-permute-start.1) | collective-permute-done | bytes 131104 | tf_op jit(solution)/shard_map/ppermute | solution.py:467
  143.6 15.4 %collective-permute-done = bf16[1,64,1024]{2,1,0:T(8,128)(2,1)S(1)} collective-permute-done((bf16[1,64,1024]{2,1,0:T(8,128)(2,1)}, bf16[1,64,1024]{2,1,0:T(8,128)(2,1)S(1)}, u32[]{:S(2)}, u32[]{:S(2)}) %collective-permute-start) | collective-permute-done | bytes 131104 | tf_op jit(solution)/shard_map/ppermute | solution.py:467
  159.0 0.7 copy.15
  159.7 0.7 copy.16
Async XLA Ops:
  134.7 9.0 %collective-permute-start.1 = (bf16[1,64,1024]{2,1,0:T(8,128)(2,1)}, bf16[1,64,1024]{2,1,0:T(8,128)(2,1)S(1)}, u32[]{:S(2)}, u32[]{:S(2)}) collective-permute-start(bf16[1,64,1024]{2,1,0:T(8,128)(2,1)} %bitcast.25), channel_id=1, source_target_pairs={{128,0},{256,128},{384,256},{0,384},{129,1},{257,129},{385,257},{1... | collective-permute-start | bytes 393224 | tf_op jit(solution)/shard_map/ppermute | solution.py:467
  136.6 22.4 %collective-permute-start = (bf16[1,64,1024]{2,1,0:T(8,128)(2,1)}, bf16[1,64,1024]{2,1,0:T(8,128)(2,1)S(1)}, u32[]{:S(2)}, u32[]{:S(2)}) collective-permute-start(bf16[1,64,1024]{2,1,0:T(8,128)(2,1)} %bitcast.24), channel_id=1, source_target_pairs={{384,0},{0,128},{128,256},{256,384},{385,1},{1,129},{129,257},{257... | collective-permute-start | bytes 393224 | tf_op jit(solution)/shard_map/ppermute | solution.py:467
